TPU v7x, 256 devices: a whole 4x4x8 slice. The times are simulated.
256 devices in a mesh: row: 32 (over z, y), col: 8 (over x, core).
Axes of the slice: x: 4, y: 4, z: 8, core: 2. Of those that a mesh axis runs over, the one named last changes fastest.
Arguments:
- anc_factor: float32 [32768, 8192], P('row', 'col'), may hold values from -0.046875 to 0.046875
- anc_solution: float32 [128, 49152], P('col', 'row'), may hold values from -6 to 6
- slot_row: int32 [32768], P('row'), may hold values from 0 to 1535, as said below
- tile_count: int32 [32], P('row'), may hold values from 2 to 8, as said below
- lower_factor: float32 [8, 1024, 8192], P(None, 'row', 'col'), may hold values from -0.109375 to 0.109375
- diag_inverse: float32 [8, 1024, 1024], P('col'), may hold values from -1.5 to 1.5, as said below
- rhs: float32 [128, 8192], P('row', 'col'), may hold values from -6 to 6
Outputs:
- solution: float32 [128, 8192], P('row', 'col')
Inputs may be any that keep to these rules, and one draw needn't show every extreme that they name: `slot_row`: within each aligned block of 1024 entries the values are distinct, and some block holds 1535. `tile_count`: some entry equals 8 in every draw. Each block diag_inverse[t] is lower triangular with a positive diagonal.
All inputs are finite; a program needn't handle non-finite values.
Results may differ from a plain program's by a relative error of at most 0.0001.
Values sent between devices are 32-bit elements; how exact they have to be, the bound alone decides.
No kernel may reach another device: no remote copies, remote signals or barrier semaphores. Data moves between devices by JAX's collectives and lax.ppermute only.
A program may use at most 64 MiB of HBM per device.

v0:
```python
import jax
import jax.numpy as jnp
from jax import lax
from jax.sharding import PartitionSpec as P

TILE = 128


def broadcast(array, axis, root):
    mine = lax.axis_index(axis) == root
    return lax.psum(jnp.where(mine, array, jnp.zeros_like(array)), axis)


def on_device(anc_factor, anc_solution, slot_row, tile_count, lower_factor, diag_inverse, rhs):
    highest = lax.Precision.HIGHEST
    column_index = lax.axis_index("col")
    panels = lower_factor.shape[0]
    rows_local = lower_factor.shape[1]
    slot_total = slot_row.shape[0]
    alive_mask = (jnp.arange(slot_total) < tile_count[0] * TILE).astype(jnp.float32)
    chosen = (
        jnp.take(lax.all_gather(anc_solution, "col", axis=0, tiled=True), slot_row, axis=1)
        * alive_mask[None, :]
    )
    ancestor_term = jnp.dot(
        chosen, anc_factor, precision=highest, preferred_element_type=jnp.float32
    )
    reduced = rhs - lax.psum_scatter(ancestor_term, "row", scatter_dimension=0, tiled=True)
    pending = jnp.zeros_like(reduced)
    result = jnp.zeros_like(reduced)
    panel_mask = (jnp.arange(panels) > column_index).astype(jnp.float32)
    lower_masked = lower_factor * panel_mask[:, None, None]
    lower_flat = lower_masked.reshape(panels * rows_local, lower_factor.shape[2])
    all_rhs = anc_solution.shape[0] * lax.axis_size("col")
    known_rows = jnp.zeros((all_rhs, panels * rows_local), jnp.float32)
    for target in range(panels - 1, -1, -1):
        if target < panels - 1:
            partial_sum = jnp.dot(
                known_rows, lower_flat, precision=highest, preferred_element_type=jnp.float32
            )
            pending = lax.psum_scatter(partial_sum, "row", scatter_dimension=0, tiled=True)
        solved = jnp.dot(
            reduced - pending,
            diag_inverse[0],
            precision=highest,
            preferred_element_type=jnp.float32,
        )
        result = jnp.where(column_index == target, solved, result)
        if target > 0:
            spread_rows = lax.all_to_all(solved, "row", split_axis=1, concat_axis=0, tiled=True)
            owner_rows = broadcast(spread_rows, "col", target)
            known_rows = known_rows.at[:, target * rows_local : (target + 1) * rows_local].set(
                owner_rows
            )
    return result


def solution(mesh):
    in_specs = (
        P("row", "col"),
        P("col", "row"),
        P("row"),
        P("row"),
        P(None, "row", "col"),
        P("col", None, None),
        P("row", "col"),
    )
    out_specs = P("row", "col")
    return jax.shard_map(
        on_device, mesh=mesh, in_specs=in_specs, out_specs=out_specs, check_vma=False
    )
```

profile of v0, /device:TPU:2, one launch (start us, length us, event | category | flops | bytes accessed | tf_op | source)
XLA Modules:
  0.0 1519.6 jit_solution(10085805310040251316)
XLA Ops:
  8.6 13.7 all_gather.3
  25.3 5.8 fusion.19
  32.4 150.3 %all-reduce.18.cloned.1.call-done = f32[128,1024]{1,0:T(8,128)} async-done(((f32[128,1024]{1,0:T(8,128)}), f32[128,1024]{1,0:T(8,128)}) %all-reduce.18.cloned.1.call-update) | async-done | bytes 524304
  188.7 5.6 all-to-all-start
  194.5 9.4 all-to-all-done
  205.4 21.0 %psum.49 = f32[128,32]{1,0:T(8,128)S(1)} all-reduce(f32[128,32]{1,0:T(8,128)S(1)} %bitcast.107), channel_id=1, replica_groups=mesh['row'=32,'col'=8] {'col'}, use_global_device_ids=true, to_apply=%region_1.2 | all-reduce | flops 4096 | bytes 32768 | tf_op jit(solution)/shard_map/psum | solution.py:11
  227.9 144.0 %all-reduce.20.cloned.1.call-done = f32[128,1024]{1,0:T(8,128)} async-done(((f32[128,1024]{1,0:T(8,128)}), f32[128,1024]{1,0:T(8,128)}) %all-reduce.20.cloned.1.call-update) | async-done | bytes 524304
  377.1 5.6 all-to-all-start.1
  383.5 8.8 all-to-all-done.1
  393.2 21.2 %psum.50 = f32[128,32]{1,0:T(8,128)S(1)} all-reduce(f32[128,32]{1,0:T(8,128)S(1)} %bitcast.108), channel_id=1, replica_groups=mesh['row'=32,'col'=8] {'col'}, use_global_device_ids=true, to_apply=%region_4.5 | all-reduce | flops 4096 | bytes 32768 | tf_op jit(solution)/shard_map/psum | solution.py:11
  417.2 144.0 %all-reduce.22.cloned.1.call-done = f32[128,1024]{1,0:T(8,128)} async-done(((f32[128,1024]{1,0:T(8,128)}), f32[128,1024]{1,0:T(8,128)}) %all-reduce.22.cloned.1.call-update) | async-done | bytes 524304
  566.4 5.6 all-to-all-start.2
  572.7 8.9 all-to-all-done.2
  582.5 21.0 %psum.51 = f32[128,32]{1,0:T(8,128)S(1)} all-reduce(f32[128,32]{1,0:T(8,128)S(1)} %bitcast.109), channel_id=1, replica_groups=mesh['row'=32,'col'=8] {'col'}, use_global_device_ids=true, to_apply=%region_7.8 | all-reduce | flops 4096 | bytes 32768 | tf_op jit(solution)/shard_map/psum | solution.py:11
  606.4 144.0 %all-reduce.24.cloned.1.call-done = f32[128,1024]{1,0:T(8,128)} async-done(((f32[128,1024]{1,0:T(8,128)}), f32[128,1024]{1,0:T(8,128)}) %all-reduce.24.cloned.1.call-update) | async-done | bytes 524304
  755.5 5.6 all-to-all-start.3
  761.8 8.9 all-to-all-done.3
  771.6 21.0 %psum.52 = f32[128,32]{1,0:T(8,128)S(1)} all-reduce(f32[128,32]{1,0:T(8,128)S(1)} %bitcast.110), channel_id=1, replica_groups=mesh['row'=32,'col'=8] {'col'}, use_global_device_ids=true, to_apply=%region_10.11 | all-reduce | flops 4096 | bytes 32768 | tf_op jit(solution)/shard_map/psum | solution.py:11
  795.3 144.0 %all-reduce.26.cloned.1.call-done = f32[128,1024]{1,0:T(8,128)} async-done(((f32[128,1024]{1,0:T(8,128)}), f32[128,1024]{1,0:T(8,128)}) %all-reduce.26.cloned.1.call-update) | async-done | bytes 524304
  944.4 5.8 all-to-all-start.4
  950.9 8.9 all-to-all-done.4
  960.7 21.0 %psum.53 = f32[128,32]{1,0:T(8,128)S(1)} all-reduce(f32[128,32]{1,0:T(8,128)S(1)} %bitcast.111), channel_id=1, replica_groups=mesh['row'=32,'col'=8] {'col'}, use_global_device_ids=true, to_apply=%region_13.14 | all-reduce | flops 4096 | bytes 32768 | tf_op jit(solution)/shard_map/psum | solution.py:11
  984.9 144.0 %all-reduce.28.cloned.1.call-done = f32[128,1024]{1,0:T(8,128)} async-done(((f32[128,1024]{1,0:T(8,128)}), f32[128,1024]{1,0:T(8,128)}) %all-reduce.28.cloned.1.call-update) | async-done | bytes 524304
  1134.0 5.6 all-to-all-start.5
  1140.3 8.9 all-to-all-done.5
  1150.1 21.0 %psum.54 = f32[128,32]{1,0:T(8,128)S(1)} all-reduce(f32[128,32]{1,0:T(8,128)S(1)} %bitcast.112), channel_id=1, replica_groups=mesh['row'=32,'col'=8] {'col'}, use_global_device_ids=true, to_apply=%region_16.17 | all-reduce | flops 4096 | bytes 32768 | tf_op jit(solution)/shard_map/psum | solution.py:11
  1174.3 144.0 %all-reduce.30.cloned.1.call-done = f32[128,1024]{1,0:T(8,128)} async-done(((f32[128,1024]{1,0:T(8,128)}), f32[128,1024]{1,0:T(8,128)}) %all-reduce.30.cloned.1.call-update) | async-done | bytes 524304
  1323.4 5.6 all-to-all-start.6
  1329.8 8.9 all-to-all-done.6
  1339.5 21.3 %psum.55 = f32[128,32]{1,0:T(8,128)S(1)} all-reduce(f32[128,32]{1,0:T(8,128)S(1)} %bitcast.113), channel_id=1, replica_groups=mesh['row'=32,'col'=8] {'col'}, use_global_device_ids=true, to_apply=%region_19.20 | all-reduce | flops 4096 | bytes 32768 | tf_op jit(solution)/shard_map/psum | solution.py:11
  1364.0 143.9 %all-reduce.32.cloned.1.call-done = f32[128,1024]{1,0:T(8,128)} async-done(((f32[128,1024]{1,0:T(8,128)}), f32[128,1024]{1,0:T(8,128)}) %all-reduce.32.cloned.1.call-update) | async-done | bytes 524304
  1507.9 4.9 fusion.16
  (106 shorter events, 72.5 us)
Async XLA Ops:
  6.5 176.2 %all-reduce.18.cloned.1.call-start = ((), (), s32[]{:S(2)}) async-start(), calls=%async_computation.7 | async-start | bytes 1048576
  22.5 8.7 copy-start.2
  22.5 160.3 %copy-start.1 = (f32[4,1024]{1,0:T(4,128)S(1)}, f32[4,1024]{1,0:T(4,128)}, u32[]{:S(2)}) copy-start(f32[4,1024]{1,0:T(4,128)} %param.27) | copy-start | bytes 49156
  25.3 168.9 %copy-start = (f32[8,32,1024]{2,1,0:T(8,128)S(1)}, f32[8,32,1024]{2,1,0:T(8,128)}, u32[]{:S(2)}) copy-start(f32[8,32,1024]{2,1,0:T(8,128)} %param.25) | copy-start | bytes 3145732
  188.7 15.2 %all-to-all-start = ((f32[32,1,128]{2,1,0:T(1,128)}), f32[32,1,128]{2,1,0:T(1,128)S(1)}, u32[]{:S(2)}, u32[]{:S(2)}) async-start(f32[32,1,128]{2,1,0:T(1,128)} %reshape.244), calls=%async_computation | async-start | bytes 32768 | tf_op jit(solution)/shard_map/all_to_all | solution.py:50
  194.2 177.7 %all-reduce.20.cloned.1.call-start = ((), (), s32[]{:S(2)}) async-start(), calls=%async_computation.8 | async-start | bytes 1048576
  377.1 15.2 %all-to-all-start.1 = ((f32[32,1,128]{2,1,0:T(1,128)}), f32[32,1,128]{2,1,0:T(1,128)S(1)}, u32[]{:S(2)}, u32[]{:S(2)}) async-start(f32[32,1,128]{2,1,0:T(1,128)} %reshape.246), calls=%async_computation.1 | async-start | bytes 32768 | tf_op jit(solution)/shard_map/all_to_all | solution.py:50
  382.7 178.6 %all-reduce.22.cloned.1.call-start = ((), (), s32[]{:S(2)}) async-start(), calls=%async_computation.9 | async-start | bytes 1048576
  566.4 15.2 %all-to-all-start.2 = ((f32[32,1,128]{2,1,0:T(1,128)}), f32[32,1,128]{2,1,0:T(1,128)S(1)}, u32[]{:S(2)}, u32[]{:S(2)}) async-start(f32[32,1,128]{2,1,0:T(1,128)} %reshape.248), calls=%async_computation.2 | async-start | bytes 32768 | tf_op jit(solution)/shard_map/all_to_all | solution.py:50
  571.9 178.4 %all-reduce.24.cloned.1.call-start = ((), (), s32[]{:S(2)}) async-start(), calls=%async_computation.10 | async-start | bytes 1048576
  755.5 15.2 %all-to-all-start.3 = ((f32[32,1,128]{2,1,0:T(1,128)}), f32[32,1,128]{2,1,0:T(1,128)S(1)}, u32[]{:S(2)}, u32[]{:S(2)}) async-start(f32[32,1,128]{2,1,0:T(1,128)} %reshape.250), calls=%async_computation.3 | async-start | bytes 32768 | tf_op jit(solution)/shard_map/all_to_all | solution.py:50
  761.1 178.2 %all-reduce.26.cloned.1.call-start = ((), (), s32[]{:S(2)}) async-start(), calls=%async_computation.11 | async-start | bytes 1048576
  944.4 15.5 %all-to-all-start.4 = ((f32[32,1,128]{2,1,0:T(1,128)}), f32[32,1,128]{2,1,0:T(1,128)S(1)}, u32[]{:S(2)}, u32[]{:S(2)}) async-start(f32[32,1,128]{2,1,0:T(1,128)} %reshape.252), calls=%async_computation.4 | async-start | bytes 32768 | tf_op jit(solution)/shard_map/all_to_all | solution.py:50
  950.2 178.7 %all-reduce.28.cloned.1.call-start = ((), (), s32[]{:S(2)}) async-start(), calls=%async_computation.12 | async-start | bytes 1048576
  1134.0 15.2 %all-to-all-start.5 = ((f32[32,1,128]{2,1,0:T(1,128)}), f32[32,1,128]{2,1,0:T(1,128)S(1)}, u32[]{:S(2)}, u32[]{:S(2)}) async-start(f32[32,1,128]{2,1,0:T(1,128)} %reshape.254), calls=%async_computation.5 | async-start | bytes 32768 | tf_op jit(solution)/shard_map/all_to_all | solution.py:50
  1139.5 178.7 %all-reduce.30.cloned.1.call-start = ((), (), s32[]{:S(2)}) async-start(), calls=%async_computation.13 | async-start | bytes 1048576
  1323.4 15.2 %all-to-all-start.6 = ((f32[32,1,128]{2,1,0:T(1,128)}), f32[32,1,128]{2,1,0:T(1,128)S(1)}, u32[]{:S(2)}, u32[]{:S(2)}) async-start(f32[32,1,128]{2,1,0:T(1,128)} %reshape.256), calls=%async_computation.6 | async-start | bytes 32768 | tf_op jit(solution)/shard_map/all_to_all | solution.py:50
  1329.0 178.9 %all-reduce.32.cloned.1.call-start = ((), (), s32[]{:S(2)}) async-start(), calls=%async_computation.14 | async-start | bytes 1048576
Sparse Core Ops, SparseCore 0:
  31.3 151.4 all-reduce.17
  228.0 143.8 all-reduce.19
  417.4 143.8 all-reduce.21
  606.5 143.7 all-reduce.23
  795.4 143.7 all-reduce.25
  985.0 143.7 all-reduce.27
  1174.4 143.8 all-reduce.29
  1364.1 143.7 all-reduce.31
where the time goes:
time: 1520 us
  waiting for transfers between devices  1220 us (80%)
  blocking collectives  161 us (11%)
  matrix products  51.4 us (3%)
  starting transfers between devices  39.4 us (3%)
  other arithmetic  16.3 us (1%)
  between operations  15.4 us (1%)
    unnamed x16, waiting for transfers between devices  1160 us
    psum x7, blocking collectives, broadcast(): return lax.psum(jnp.where(mine, array, jnp.zeros_like(array)), axis)  147 us
    all_to_all x7, waiting for transfers between devices, on_device(): lax.all_to_all(solved, 'row', split_axis=1, concat_axis=0, tiled=True)  62.8 us
    all_to_all x7, starting transfers between devices, on_device(): lax.all_to_all(solved, 'row', split_axis=1, concat_axis=0, tiled=True)  39.1 us
    dot_general x8, matrix products, on_device(): jnp.dot(reduced - pending, diag_inverse[0], precision=highest, preferred_...  34.9 us
  transfers between devices with their start and end apart: 15, of which 15 were waited for; matrix products, arithmetic and copies ran while one was open for 0% of the time, Pallas kernels for 0%

commit v1 on v0

--- a/solution.py
+++ b/solution.py
@@ -6,9 +6,15 @@
 TILE = 128
 
 
+def gather_and_add(value, name):
+    blocks = lax.all_gather(value, name, axis=0, tiled=False)
+    acc = blocks.sum(axis=0)
+    return acc
+
+
 def broadcast(array, axis, root):
     mine = lax.axis_index(axis) == root
-    return lax.psum(jnp.where(mine, array, jnp.zeros_like(array)), axis)
+    return gather_and_add(jnp.where(mine, array, jnp.zeros_like(array)), axis)
 
 
 def on_device(anc_factor, anc_solution, slot_row, tile_count, lower_factor, diag_inverse, rhs):

time: 1520 us -> 1450 us (0.954)
  blocking collectives: 161 us -> 103 us
    psum x7 -> x0, blocking collectives: 147 us -> none  [broadcast(): return lax.psum(jnp.where(mine, array, jnp.zeros_like(array)), axis)]
    all_gather x0 -> x7, blocking collectives: none -> 89.7 us  [gather_and_add(): blocks = lax.all_gather(value, name, axis=0, tiled=False)]
where the time goes in v1:
time: 1450 us
  waiting for transfers between devices  1220 us (84%)
  blocking collectives  103 us (7%)
  matrix products  51.3 us (4%)
  starting transfers between devices  39.4 us (3%)
  other arithmetic  16.1 us (1%)
  between operations  15.3 us (1%)
    unnamed x16, waiting for transfers between devices  1150 us
    all_gather x7, blocking collectives, gather_and_add(): blocks = lax.all_gather(value, name, axis=0, tiled=False)  89.7 us
    all_to_all x7, waiting for transfers between devices, on_device(): lax.all_to_all(solved, 'row', split_axis=1, concat_axis=0, tiled=True)  62.9 us
    all_to_all x7, starting transfers between devices, on_device(): lax.all_to_all(solved, 'row', split_axis=1, concat_axis=0, tiled=True)  39.1 us
    dot_general x8, matrix products, on_device(): jnp.dot(reduced - pending, diag_inverse[0], precision=highest, preferred_...  34.9 us
  transfers between devices with their start and end apart: 15, of which 15 were waited for; matrix products, arithmetic and copies ran while one was open for 0% of the time, Pallas kernels for 0%

profile of v1, /device:TPU:2, one launch (start us, length us, event | category | flops | bytes accessed | tf_op | source)
XLA Modules:
  0.0 1452.2 jit_solution(14312488459196534371)
XLA Ops:
  8.6 13.7 all_gather.31
  25.3 5.8 fusion.19
  32.4 150.3 %all-reduce.18.cloned.1.call-done = f32[128,1024]{1,0:T(8,128)} async-done(((f32[128,1024]{1,0:T(8,128)}), f32[128,1024]{1,0:T(8,128)}) %all-reduce.18.cloned.1.call-update) | async-done | bytes 524304
  188.7 5.6 all-to-all-start
  194.5 9.4 all-to-all-done
  205.4 12.8 all_gather.32
  219.7 143.2 %all-reduce.20.cloned.1.call-done = f32[128,1024]{1,0:T(8,128)} async-done(((f32[128,1024]{1,0:T(8,128)}), f32[128,1024]{1,0:T(8,128)}) %all-reduce.20.cloned.1.call-update) | async-done | bytes 524304
  368.1 5.6 all-to-all-start.1
  374.4 8.9 all-to-all-done.1
  384.2 12.9 all_gather.33
  399.4 143.1 %all-reduce.22.cloned.1.call-done = f32[128,1024]{1,0:T(8,128)} async-done(((f32[128,1024]{1,0:T(8,128)}), f32[128,1024]{1,0:T(8,128)}) %all-reduce.22.cloned.1.call-update) | async-done | bytes 524304
  547.7 5.6 all-to-all-start.2
  554.0 8.9 all-to-all-done.2
  563.9 12.8 all_gather.34
  578.9 143.1 %all-reduce.24.cloned.1.call-done = f32[128,1024]{1,0:T(8,128)} async-done(((f32[128,1024]{1,0:T(8,128)}), f32[128,1024]{1,0:T(8,128)}) %all-reduce.24.cloned.1.call-update) | async-done | bytes 524304
  727.2 5.6 all-to-all-start.3
  733.5 8.9 all-to-all-done.3
  743.3 12.8 all_gather.35
  758.3 143.1 %all-reduce.26.cloned.1.call-done = f32[128,1024]{1,0:T(8,128)} async-done(((f32[128,1024]{1,0:T(8,128)}), f32[128,1024]{1,0:T(8,128)}) %all-reduce.26.cloned.1.call-update) | async-done | bytes 524304
  906.6 5.8 all-to-all-start.4
  913.2 8.9 all-to-all-done.4
  923.0 12.8 all_gather.36
  938.0 143.1 %all-reduce.28.cloned.1.call-done = f32[128,1024]{1,0:T(8,128)} async-done(((f32[128,1024]{1,0:T(8,128)}), f32[128,1024]{1,0:T(8,128)}) %all-reduce.28.cloned.1.call-update) | async-done | bytes 524304
  1086.3 5.6 all-to-all-start.5
  1092.6 8.9 all-to-all-done.5
  1102.5 12.8 all_gather.37
  1117.5 143.2 %all-reduce.30.cloned.1.call-done = f32[128,1024]{1,0:T(8,128)} async-done(((f32[128,1024]{1,0:T(8,128)}), f32[128,1024]{1,0:T(8,128)}) %all-reduce.30.cloned.1.call-update) | async-done | bytes 524304
  1265.8 5.6 all-to-all-start.6
  1272.2 8.9 all-to-all-done.6
  1282.0 13.0 all_gather.38
  1297.3 143.1 %all-reduce.32.cloned.1.call-done = f32[128,1024]{1,0:T(8,128)} async-done(((f32[128,1024]{1,0:T(8,128)}), f32[128,1024]{1,0:T(8,128)}) %all-reduce.32.cloned.1.call-update) | async-done | bytes 524304
  1440.4 4.9 fusion.16
  (114 shorter events, 68.4 us)
Async XLA Ops:
  6.5 176.2 %all-reduce.18.cloned.1.call-start = ((), (), s32[]{:S(2)}) async-start(), calls=%async_computation.7 | async-start | bytes 1048576
  22.5 8.7 copy-start.2
  22.5 160.3 %copy-start.1 = (f32[4,1024]{1,0:T(4,128)S(1)}, f32[4,1024]{1,0:T(4,128)}, u32[]{:S(2)}) copy-start(f32[4,1024]{1,0:T(4,128)} %param.27) | copy-start | bytes 49156
  25.3 168.9 %copy-start = (f32[8,32,1024]{2,1,0:T(8,128)S(1)}, f32[8,32,1024]{2,1,0:T(8,128)}, u32[]{:S(2)}) copy-start(f32[8,32,1024]{2,1,0:T(8,128)} %param.25) | copy-start | bytes 3145732
  188.7 15.2 %all-to-all-start = ((f32[32,1,128]{2,1,0:T(1,128)}), f32[32,1,128]{2,1,0:T(1,128)S(1)}, u32[]{:S(2)}, u32[]{:S(2)}) async-start(f32[32,1,128]{2,1,0:T(1,128)} %reshape.314), calls=%async_computation | async-start | bytes 32768 | tf_op jit(solution)/shard_map/all_to_all | solution.py:56
  194.2 168.7 %all-reduce.20.cloned.1.call-start = ((), (), s32[]{:S(2)}) async-start(), calls=%async_computation.8 | async-start | bytes 1048576
  368.1 15.2 %all-to-all-start.1 = ((f32[32,1,128]{2,1,0:T(1,128)}), f32[32,1,128]{2,1,0:T(1,128)S(1)}, u32[]{:S(2)}, u32[]{:S(2)}) async-start(f32[32,1,128]{2,1,0:T(1,128)} %reshape.316), calls=%async_computation.1 | async-start | bytes 32768 | tf_op jit(solution)/shard_map/all_to_all | solution.py:56
  373.6 168.9 %all-reduce.22.cloned.1.call-start = ((), (), s32[]{:S(2)}) async-start(), calls=%async_computation.9 | async-start | bytes 1048576
  547.7 15.2 %all-to-all-start.2 = ((f32[32,1,128]{2,1,0:T(1,128)}), f32[32,1,128]{2,1,0:T(1,128)S(1)}, u32[]{:S(2)}, u32[]{:S(2)}) async-start(f32[32,1,128]{2,1,0:T(1,128)} %reshape.318), calls=%async_computation.2 | async-start | bytes 32768 | tf_op jit(solution)/shard_map/all_to_all | solution.py:56
  553.3 168.8 %all-reduce.24.cloned.1.call-start = ((), (), s32[]{:S(2)}) async-start(), calls=%async_computation.10 | async-start | bytes 1048576
  727.2 15.2 %all-to-all-start.3 = ((f32[32,1,128]{2,1,0:T(1,128)}), f32[32,1,128]{2,1,0:T(1,128)S(1)}, u32[]{:S(2)}, u32[]{:S(2)}) async-start(f32[32,1,128]{2,1,0:T(1,128)} %reshape.320), calls=%async_computation.3 | async-start | bytes 32768 | tf_op jit(solution)/shard_map/all_to_all | solution.py:56
  732.7 168.8 %all-reduce.26.cloned.1.call-start = ((), (), s32[]{:S(2)}) async-start(), calls=%async_computation.11 | async-start | bytes 1048576
  906.6 15.5 %all-to-all-start.4 = ((f32[32,1,128]{2,1,0:T(1,128)}), f32[32,1,128]{2,1,0:T(1,128)S(1)}, u32[]{:S(2)}, u32[]{:S(2)}) async-start(f32[32,1,128]{2,1,0:T(1,128)} %reshape.322), calls=%async_computation.4 | async-start | bytes 32768 | tf_op jit(solution)/shard_map/all_to_all | solution.py:56
  912.4 168.8 %all-reduce.28.cloned.1.call-start = ((), (), s32[]{:S(2)}) async-start(), calls=%async_computation.12 | async-start | bytes 1048576
  1086.3 15.2 %all-to-all-start.5 = ((f32[32,1,128]{2,1,0:T(1,128)}), f32[32,1,128]{2,1,0:T(1,128)S(1)}, u32[]{:S(2)}, u32[]{:S(2)}) async-start(f32[32,1,128]{2,1,0:T(1,128)} %reshape.324), calls=%async_computation.5 | async-start | bytes 32768 | tf_op jit(solution)/shard_map/all_to_all | solution.py:56
  1091.9 168.8 %all-reduce.30.cloned.1.call-start = ((), (), s32[]{:S(2)}) async-start(), calls=%async_computation.13 | async-start | bytes 1048576
  1265.8 15.2 %all-to-all-start.6 = ((f32[32,1,128]{2,1,0:T(1,128)}), f32[32,1,128]{2,1,0:T(1,128)S(1)}, u32[]{:S(2)}, u32[]{:S(2)}) async-start(f32[32,1,128]{2,1,0:T(1,128)} %reshape.326), calls=%async_computation.6 | async-start | bytes 32768 | tf_op jit(solution)/shard_map/all_to_all | solution.py:56
  1271.4 169.0 %all-reduce.32.cloned.1.call-start = ((), (), s32[]{:S(2)}) async-start(), calls=%async_computation.14 | async-start | bytes 1048576
Sparse Core Ops, SparseCore 0:
  31.3 151.4 all-reduce.17
  219.8 143.0 all-reduce.19
  399.5 142.9 all-reduce.21
  579.0 142.9 all-reduce.23
  758.5 142.9 all-reduce.25
  938.2 142.9 all-reduce.27
  1117.6 143.0 all-reduce.29
  1297.4 142.9 all-reduce.31
